TPU v7x, 512 devices: a whole 4x8x8 slice. The times are simulated.
512 devices in a mesh: dp: 16 (over z, core), ctx: 32 (over y, x).
Axes of the slice: x: 4, y: 8, z: 8, core: 2. Of those that a mesh axis runs over, the one named last changes fastest.
Arguments:
- query_in: bfloat16 [16, 8192, 1280], P('dp', 'ctx'), may hold values from -150 to 150
- key_in: bfloat16 [16, 8192, 1280], P('dp', 'ctx'), may hold values from -16 to 16
- value_in: bfloat16 [16, 8192, 1280], P('dp', 'ctx'), may hold values from -6 to 6
- grad_out: bfloat16 [16, 8192, 1280], P('dp', 'ctx'), may hold values from -6 to 6
- key_blocks: int32 [10, 32, 6], P(None, 'ctx'), may hold values from 0 to 63, as said below
- sink_logits: float32 [10], replicated, may hold values from 3 to 8
Outputs:
- grad_query: bfloat16 [16, 8192, 1280], P('dp', 'ctx')
- grad_key: bfloat16 [16, 8192, 1280], P('dp', 'ctx')
- grad_value: bfloat16 [16, 8192, 1280], P('dp', 'ctx')
- grad_sink: float32 [10], replicated
Inputs may be any that keep to these rules, and one draw needn't show every extreme that they name: `key_blocks`: block b holds tokens 128 b to 128 b + 127. The 6 entries of one head and segment are distinct, and none falls in the aligned group of 256 tokens that holds the segment. Counting all heads, entries and segments of one aligned group of 256 tokens, at most 2 entries fall in any one other aligned group of 256 tokens, and every group reaches 2 with some other group in every draw.
All inputs are finite; a program needn't handle non-finite values.
Results may differ from a plain program's by a relative error of at most 0.012.
Values may be sent and summed in bfloat16 or wider, within the bound.
A program may use at most 64 MiB of HBM per device.

v0:
```python
from functools import partial
import math
import jax
import jax.numpy as jnp
from jax import lax
from jax.sharding import PartitionSpec as P

BLOCK = 128


def slot_layout(block_rows, groups, per_group, capacity):
    head_count, segments, listed = block_rows.shape
    ordered = jnp.transpose(block_rows, (2, 0, 1)).reshape(-1)
    head_ids = jnp.broadcast_to(
        jnp.arange(head_count, dtype=jnp.int32)[None, :, None], (listed, head_count, segments)
    ).reshape(-1)
    owners = ordered // per_group
    req_codes = head_ids * per_group + ordered % per_group
    positions = jnp.arange(ordered.shape[0], dtype=jnp.int32)
    earlier = (owners[:, None] == owners[None, :]) & (positions[None, :] < positions[:, None])
    places = owners * capacity + jnp.sum(earlier.astype(jnp.int32), axis=1)
    targets = jnp.arange(groups * capacity, dtype=jnp.int32)
    matched = places[None, :] == targets[:, None]
    filled = jnp.any(matched, axis=1)
    source_ids = jnp.sum(jnp.where(matched, positions[None, :], 0), axis=1)
    sent_codes = jnp.where(filled, jnp.sum(jnp.where(matched, req_codes[None, :], 0), axis=1), -1)
    return (places, filled, source_ids, sent_codes.reshape(groups, capacity))


def log_total(scores, sink_grp):
    sink_side = sink_grp[:, None, None]
    row_top = jnp.maximum(jnp.max(scores, axis=-1), sink_side)
    row_total = jnp.exp(sink_side - row_top) + jnp.sum(
        jnp.exp(scores - row_top[..., None]), axis=-1
    )
    return row_top + jnp.log(row_total)


def forward_group(inputs, scaling):
    query_grp, local_kv, remote_kv, sink_grp = inputs
    head_dim = query_grp.shape[-1]
    kv_all = jnp.concatenate([local_kv, remote_kv], axis=2)
    scores = (
        jnp.einsum(
            "gsqd,gskd->gsqk", query_grp, kv_all[..., :head_dim], preferred_element_type=jnp.float32
        )
        * scaling
    )
    log_norm = log_total(scores, sink_grp)
    prob_bf = jnp.exp(scores - log_norm[..., None]).astype(jnp.bfloat16)
    attended = jnp.einsum(
        "gsqk,gskd->gsqd", prob_bf, kv_all[..., head_dim:], preferred_element_type=jnp.float32
    )
    return (attended.astype(jnp.bfloat16), log_norm)


def backward_group(inputs, scaling, seg_len):
    query_grp, local_kv, remote_kv, sink_grp, grad_grp, attended, log_norm = inputs
    head_dim = query_grp.shape[-1]
    kv_all = jnp.concatenate([local_kv, remote_kv], axis=2)
    scores = (
        jnp.einsum(
            "gsqd,gskd->gsqk", query_grp, kv_all[..., :head_dim], preferred_element_type=jnp.float32
        )
        * scaling
    )
    weights = jnp.exp(scores - log_norm[..., None])
    prob_bf = weights.astype(jnp.bfloat16)
    row_delta = jnp.sum(grad_grp.astype(jnp.float32) * attended.astype(jnp.float32), axis=-1)
    dprobs = jnp.einsum(
        "gsqd,gskd->gsqk", grad_grp, kv_all[..., head_dim:], preferred_element_type=jnp.float32
    )
    dscores = (weights * (dprobs - row_delta[..., None])).astype(jnp.bfloat16)
    grad_q = (
        jnp.einsum(
            "gsqk,gskd->gsqd", dscores, kv_all[..., :head_dim], preferred_element_type=jnp.float32
        )
        * scaling
    )
    key_terms = (
        jnp.einsum("gsqk,gsqd->gskd", dscores, query_grp, preferred_element_type=jnp.float32)
        * scaling
    )
    value_terms = jnp.einsum(
        "gsqk,gsqd->gskd", prob_bf, grad_grp, preferred_element_type=jnp.float32
    )
    all_terms = jnp.concatenate([key_terms, value_terms], axis=-1)
    sink_part = -jnp.sum(jnp.exp(sink_grp[:, None, None] - log_norm) * row_delta, axis=(1, 2))
    return (
        grad_q.astype(jnp.bfloat16),
        all_terms[:, :, :seg_len],
        all_terms[:, :, seg_len:].astype(jnp.bfloat16),
        sink_part,
    )


def body(query_in, key_in, value_in, grad_out, key_blocks, sink_logits):
    groups = lax.axis_size("ctx")
    head_count = sink_logits.shape[0]
    tok_dev = query_in.shape[1]
    head_dim = query_in.shape[2] // head_count
    seg_per_dev = key_blocks.shape[1]
    listed = key_blocks.shape[2]
    seg_len = tok_dev // seg_per_dev
    per_group = tok_dev // BLOCK
    requests = head_count * seg_per_dev * listed
    capacity = (requests + groups - 2) // (groups - 1)
    scaling = 1.0 / math.sqrt(head_dim)
    pair_heads = 2
    pair_count = head_count // pair_heads
    double_dim = 2 * head_dim
    places, filled, source_ids, sent_codes = slot_layout(key_blocks, groups, per_group, capacity)
    recv_codes = lax.all_to_all(sent_codes, "ctx", split_axis=0, concat_axis=0, tiled=True)
    local_kv = jnp.concatenate(
        [
            key_in[0].reshape(per_group, BLOCK, head_count, head_dim),
            value_in[0].reshape(per_group, BLOCK, head_count, head_dim),
        ],
        axis=-1,
    )
    safe_codes = jnp.maximum(recv_codes, 0)
    payload = local_kv[safe_codes % per_group, :, safe_codes // per_group, :]

    def arrange_remote(fetched):
        flat_slots = fetched.reshape(groups * capacity, BLOCK, double_dim)
        remote_rows = flat_slots[places].reshape(listed, head_count, seg_per_dev, BLOCK, double_dim)
        remote_rows = jnp.transpose(remote_rows, (1, 2, 0, 3, 4))
        return remote_rows.reshape(pair_count, pair_heads, seg_per_dev, listed * BLOCK, double_dim)

    def to_pairs(field):
        columns = field.shape[-1]
        split = jnp.transpose(
            field.reshape(seg_per_dev, seg_len, head_count, columns), (2, 0, 1, 3)
        )
        return split.reshape(pair_count, pair_heads, seg_per_dev, seg_len, columns)

    fetched = lax.all_to_all(payload, "ctx", split_axis=0, concat_axis=0, tiled=True)
    remote_pairs = arrange_remote(fetched)
    query_pairs = to_pairs(query_in[0].reshape(tok_dev, head_count, head_dim))
    grad_pairs = to_pairs(grad_out[0].reshape(tok_dev, head_count, head_dim))
    local_pairs = to_pairs(local_kv.reshape(tok_dev, head_count, double_dim))
    sink_pairs = sink_logits.reshape(pair_count, pair_heads)
    attended, log_norm = lax.map(
        partial(forward_group, scaling=scaling),
        (query_pairs, local_pairs, remote_pairs, sink_pairs),
    )
    back_remote = arrange_remote(
        lax.all_to_all(payload, "ctx", split_axis=0, concat_axis=0, tiled=True)
    )
    grad_q, own_terms, list_terms, sink_parts = lax.map(
        partial(backward_group, scaling=scaling, seg_len=seg_len),
        (query_pairs, local_pairs, back_remote, sink_pairs, grad_pairs, attended, log_norm),
    )
    grad_query = jnp.transpose(
        grad_q.reshape(head_count, seg_per_dev, seg_len, head_dim), (1, 2, 0, 3)
    )
    grad_query = grad_query.reshape(1, tok_dev, head_count * head_dim)
    own_flat = jnp.transpose(
        own_terms.reshape(head_count, seg_per_dev, seg_len, double_dim), (1, 2, 0, 3)
    )
    own_flat = own_flat.reshape(tok_dev, head_count, double_dim)
    list_rows = jnp.transpose(
        list_terms.reshape(head_count, seg_per_dev, listed, BLOCK, double_dim), (2, 0, 1, 3, 4)
    )
    list_rows = list_rows.reshape(requests, BLOCK, double_dim)
    send_back = jnp.where(filled[:, None, None], list_rows[source_ids], jnp.zeros((), jnp.bfloat16))
    returned = lax.all_to_all(
        send_back.reshape(groups, capacity, BLOCK, double_dim),
        "ctx",
        split_axis=0,
        concat_axis=0,
        tiled=True,
    )
    selector = (
        recv_codes.reshape(-1)[:, None]
        == jnp.arange(head_count * per_group, dtype=jnp.int32)[None, :]
    ).astype(jnp.bfloat16)
    incoming = jnp.einsum(
        "pj,pbe->jbe",
        selector,
        returned.reshape(groups * capacity, BLOCK, double_dim),
        preferred_element_type=jnp.float32,
    )
    incoming = jnp.transpose(
        incoming.reshape(head_count, per_group, BLOCK, double_dim), (1, 2, 0, 3)
    )
    combined = own_flat + incoming.reshape(tok_dev, head_count, double_dim)
    grad_key = (
        combined[..., :head_dim].astype(jnp.bfloat16).reshape(1, tok_dev, head_count * head_dim)
    )
    grad_value = (
        combined[..., head_dim:].astype(jnp.bfloat16).reshape(1, tok_dev, head_count * head_dim)
    )
    grad_sink = lax.psum(sink_parts.reshape(head_count), ("dp", "ctx"))
    return (grad_query, grad_key, grad_value, grad_sink)


def solution(mesh):
    placed = (
        P("dp", "ctx", None),
        P("dp", "ctx", None),
        P("dp", "ctx", None),
        P("dp", "ctx", None),
        P(None, "ctx", None),
        P(),
    )
    return jax.shard_map(
        body,
        mesh=mesh,
        in_specs=placed,
        out_specs=(P("dp", "ctx", None), P("dp", "ctx", None), P("dp", "ctx", None), P()),
        check_vma=False,
    )
```

profile of v0, /device:TPU:27, one launch (start us, length us, event | category | flops | bytes accessed | tf_op | source)
XLA Modules:
  0.0 474.1 jit_solution(14421471684461468160)
XLA Ops:
  2.7 9.4 %all-to-all-start = ((s32[32,1,2]{2,1,0:T(1,128)}), s32[32,1,2]{2,1,0:T(1,128)S(1)}, u32[]{:S(2)}, u32[]{:S(2)}) async-start(s32[32,1,2]{2,1,0:T(1,128)} %bitcast.31), calls=%async_computation | async-start | bytes 32768 | tf_op jit(solution)/shard_map/all_to_all | solution.py:113
  12.0 1.5 reshape.729
  14.4 2.6 all-to-all-done
  17.3 2.8 gather_fusion
  20.1 8.4 %all-to-all-start.1 = ((bf16[32,2,128,256]{3,2,1,0:T(8,128)(2,1)}), bf16[32,2,128,256]{3,2,1,0:T(8,128)(2,1)}, u32[]{:S(2)}, u32[]{:S(2)}) async-start(bf16[32,2,128,256]{3,2,1,0:T(8,128)(2,1)} %bitcast.232), calls=%async_computation.1 | async-start | bytes 8388608 | tf_op jit(solution)/shard_map/all_to_all | solution.py:148
  29.9 1.1 copy.160
  30.9 2.2 copy.159
  33.2 1.5 copy.161
  34.7 83.7 %all-to-all-done.1 = bf16[32,2,128,256]{3,2,1,0:T(8,128)(2,1)} async-done(((bf16[32,2,128,256]{3,2,1,0:T(8,128)(2,1)}), bf16[32,2,128,256]{3,2,1,0:T(8,128)(2,1)}, u32[]{:S(2)}, u32[]{:S(2)}) %all-to-all-start.1) | async-done | bytes 4194336 | tf_op jit(solution)/shard_map/all_to_all | solution.py:148
  118.4 4.9 %gather_fusion.1 = bf16[60,128,256]{2,1,0:T(8,128)(2,1)} fusion(bf16[64,128,256]{2,1,0:T(8,128)(2,1)} %bitcast.36, s32[1024]{0:T(1024)S(1)} %pad_clamp_fusion.1), kind=kCustom, calls=%fused_computation.1 | custom fusion | bytes 7864560 | tf_op jit(solution)/shard_map/gather | solution.py:126
  123.2 4.4 copy.155
  127.7 28.0 %while.28 = (s32[]{:T(128)}, bf16[5,2,1,256,128]{4,3,1,2,0:T(8,128)(2,1)}, f32[5,2,1,256]{3,1,2,0:T(2,128)S(1)}, bf16[5,2,1,256,128]{4,3,1,2,0:T(8,128)(2,1)}, b...) while((s32[]{:T(128)}, ...), condition=%wide.region_6.7_spmd, body=%wide.region_3.6_spmd.sunk | while | flops 274796032 | bytes 10773141 | solution.py:143
  128.7 1.2 dynamic-slice_bitcast_fusion.9
  129.9 1.4 multiply_reduce_fusion.6
  131.9 1.2 fusion.95
  134.3 1.2 dynamic-slice_bitcast_fusion.9
  135.5 1.4 multiply_reduce_fusion.6
  137.6 1.2 fusion.95
  139.9 1.2 dynamic-slice_bitcast_fusion.9
  141.1 1.4 multiply_reduce_fusion.6
  143.2 1.2 fusion.95
  145.5 1.2 dynamic-slice_bitcast_fusion.9
  146.7 1.4 multiply_reduce_fusion.6
  148.8 1.2 fusion.95
  151.1 1.2 dynamic-slice_bitcast_fusion.9
  152.3 1.4 multiply_reduce_fusion.6
  154.4 1.2 fusion.95
  155.7 69.4 %while.29 = (s32[]{:T(128)}, bf16[5,2,1,256,128]{3,4,1,0,2:T(8,128)(2,1)}, f32[5,2,1,256,256]{3,4,1,2,0:T(8,128)}, bf16[5,2,1,768,256]{4,3,1,0,2:T(8,128)(2,1)},...) while((s32[]{:T(128)}, ...), condition=%wide.region_10.11_spmd, body=%wide.region_7.10_spmd.sunk | while | flops 680788992 | bytes 27408636 | solution.py:150
  156.8 1.1 multiply_reduce_fusion.7
  159.1 1.2 dynamic-slice_bitcast_fusion.11
  160.3 1.3 fusion.107
  163.4 1.3 fusion.110
  166.4 1.4 copy.191
  170.7 1.1 multiply_reduce_fusion.7
  173.0 1.2 dynamic-slice_bitcast_fusion.11
  174.2 1.3 fusion.107
  177.3 1.3 fusion.110
  180.3 1.4 copy.191
  186.9 1.2 dynamic-slice_bitcast_fusion.11
  188.1 1.3 fusion.107
  191.2 1.3 fusion.110
  194.2 1.4 copy.191
  198.5 1.1 multiply_reduce_fusion.7
  200.8 1.2 dynamic-slice_bitcast_fusion.11
  201.9 1.3 fusion.107
  205.1 1.3 fusion.110
  208.1 1.4 copy.191
  214.6 1.2 dynamic-slice_bitcast_fusion.11
  215.8 1.3 fusion.107
  218.9 1.3 fusion.110
  222.0 1.4 copy.191
  225.2 4.4 copy.166
  229.6 4.9 %gather_fusion.2 = bf16[64,128,256]{2,1,0:T(8,128)(2,1)} fusion(bf16[60,128,256]{2,1,0:T(8,128)(2,1)} %bitcast.231, s32[1024]{0:T(1024)S(1)} %pad_clamp_fusion), kind=kCustom, calls=%fused_computation.2 | custom fusion | bytes 8388864 | tf_op jit(solution)/shard_map/gather | solution.py:166
  234.4 9.1 %broadcast_select_fusion = bf16[32,2,128,256]{3,1,2,0:T(2,128)(2,1)} fusion(pred[32,2]{1,0:T(8,128)(4,1)S(1)} %broadcast_in_dim.98, bf16[32,2,128,256]{3,2,1,0:T(8,128)(2,1)} %bitcast.234), kind=kLoop, calls=%fused_computation.85 | loop fusion | flops 2097152 | bytes 8388672 | tf_op jit(solution)/shard_map/jit(_where)/select_n | solution.py:166
  243.5 9.7 %all-to-all-start.2 = ((bf16[32,2,128,256]{3,1,2,0:T(2,128)(2,1)}), bf16[32,2,128,256]{3,1,2,0:T(2,128)(2,1)}, u32[]{:S(2)}, u32[]{:S(2)}) async-start(bf16[32,2,128,256]{3,1,2,0:T(2,128)(2,1)} %broadcast_select_fusion), calls=%async_computation.2 | async-start | bytes 8388608 | tf_op jit(solution)/shard_map/all_to_all | solution.py:167
  254.7 188.4 %psum.7 = f32[10]{0:T(128)} all-reduce(f32[10]{0:T(128)S(1)} %reshape.704), channel_id=1, replica_groups=mesh['dp'=16,'ctx'=32] {'dp','ctx'}, use_global_device_ids=true, to_apply=%region_12.13 | all-reduce | flops 10 | bytes 80 | tf_op jit(solution)/shard_map/psum | solution.py:194
  443.0 2.2 copy.170
  445.2 8.9 %copy.168 = bf16[32,2,128,256]{3,1,0,2:T(2,128)(2,1)} copy(bf16[32,2,128,256]{3,1,2,0:T(2,128)(2,1)} %all-to-all-done.2) | data formatting | bytes 8388608 | tf_op jit(solution)/shard_map/all_to_all | solution.py:167
  454.1 7.2 %reshape.728 = bf16[64,128,256,1]{2,0,1,3:T(8,128)(2,1)} reshape(bf16[32,2,128,256]{3,1,0,2:T(2,128)(2,1)} %copy.168) | data formatting | bytes 8388608 | tf_op jit(solution)/shard_map/reshape | solution.py:181
  461.3 4.9 %fusion.56 = f32[10,2,128,256]{3,0,2,1:T(8,128)} fusion(bf16[64,128,256,1]{2,0,1,3:T(8,128)(2,1)} %reshape.728, s32[10,2]{0,1:T(2,128)S(1)} %multiply_add_fusion, s32[64]{0:T(128)S(1)} %eq.67), kind=kOutput, calls=%fused_computation.97 | convolution fusion | flops 83887360 | bytes 6816080 | tf_op jit(solution)/shard_map/pj,pbe->jbe/dot_general | solution.py:178
  466.2 3.4 copy.169
  469.6 2.2 fusion.53
  471.9 1.1 copy.172
  473.0 1.1 copy.171
  (162 shorter events, 54.6 us)
Async XLA Ops:
  0.6 0.7 copy-start
  0.6 13.0 %copy-start.3 = (bf16[1,256,1280]{2,1,0:T(8,128)(2,1)S(1)}, bf16[1,256,1280]{2,1,0:T(8,128)(2,1)}, u32[]{:S(2)}) copy-start(bf16[1,256,1280]{2,1,0:T(8,128)(2,1)} %param.12) | copy-start | bytes 1966084
  2.7 14.4 %all-to-all-start = ((s32[32,1,2]{2,1,0:T(1,128)}), s32[32,1,2]{2,1,0:T(1,128)S(1)}, u32[]{:S(2)}, u32[]{:S(2)}) async-start(s32[32,1,2]{2,1,0:T(1,128)} %bitcast.31), calls=%async_computation | async-start | bytes 32768 | tf_op jit(solution)/shard_map/all_to_all | solution.py:113
  20.1 8.6 %copy-start.2 = (bf16[1,256,1280]{2,1,0:T(8,128)(2,1)S(1)}, bf16[1,256,1280]{2,1,0:T(8,128)(2,1)}, u32[]{:S(2)}) copy-start(bf16[1,256,1280]{2,1,0:T(8,128)(2,1)} %param.11) | copy-start | bytes 1966084
  20.1 98.2 %all-to-all-start.1 = ((bf16[32,2,128,256]{3,2,1,0:T(8,128)(2,1)}), bf16[32,2,128,256]{3,2,1,0:T(8,128)(2,1)}, u32[]{:S(2)}, u32[]{:S(2)}) async-start(bf16[32,2,128,256]{3,2,1,0:T(8,128)(2,1)} %bitcast.232), calls=%async_computation.1 | async-start | bytes 8388608 | tf_op jit(solution)/shard_map/all_to_all | solution.py:148
  28.5 0.8 copy-start.5
  28.5 1.1 copy-start.4
  243.5 201.7 %all-to-all-start.2 = ((bf16[32,2,128,256]{3,1,2,0:T(2,128)(2,1)}), bf16[32,2,128,256]{3,1,2,0:T(2,128)(2,1)}, u32[]{:S(2)}, u32[]{:S(2)}) async-start(bf16[32,2,128,256]{3,1,2,0:T(2,128)(2,1)} %broadcast_select_fusion), calls=%async_computation.2 | async-start | bytes 8388608 | tf_op jit(solution)/shard_map/all_to_all | solution.py:167
  469.6 4.5 copy-start.1
where the time goes:
time: 476 us; the launch traced here: 474 us
  blocking collectives  188 us (39%)
  local copies, waits for them, and re-layouts  98.7 us (21%)
  waiting for transfers between devices  86.3 us (18%)
  matrix products  40.1 us (8%)
  other arithmetic  31.8 us (7%)
  starting transfers between devices  27.5 us (6%)
    psum x1, blocking collectives, body(): grad_sink = lax.psum(sink_parts.reshape(head_count), ('dp', 'ctx'))  188 us
    all_to_all x1, waiting for transfers between devices, body(): lax.all_to_all(payload, 'ctx', split_axis=0, concat_axis=0, tiled=True)  83.7 us
    squeeze x20, local copies, waits for them, and re-layouts, body(): lax.map(partial(forward_group, scaling=scaling), (query_pairs, local_pair...  21.6 us
    dynamic_update_slice x15, local copies, waits for them, and re-layouts, body(): lax.map(partial(backward_group, scaling=scaling, seg_len=seg_len), (query...  11.9 us
    all_to_all x1, starting transfers between devices, body(): lax.all_to_all(send_back.reshape(groups, capacity, BLOCK, double_dim), 'c...  9.72 us
  transfers between devices with their start and end apart: 3, of which 2 were waited for; matrix products, arithmetic and copies ran while one was open for 2% of the time, Pallas kernels for 0%

commit v1 on v0

--- a/solution.py
+++ b/solution.py
@@ -191,7 +191,8 @@
     grad_value = (
         combined[..., head_dim:].astype(jnp.bfloat16).reshape(1, tok_dev, head_count * head_dim)
     )
-    grad_sink = lax.psum(sink_parts.reshape(head_count), ("dp", "ctx"))
+    partial_2 = lax.psum(sink_parts.reshape(head_count), "dp")
+    grad_sink = lax.psum(partial_2, "ctx")
     return (grad_query, grad_key, grad_value, grad_sink)
 
 

time: 476 us -> 442 us (0.929)
  the two profiles are of different devices: /device:TPU:27 before, /device:TPU:354 now
where the time goes in v1:
time: 442 us; the launch traced here: 440 us
  blocking collectives  152 us (34%)
  local copies, waits for them, and re-layouts  98.7 us (22%)
  waiting for transfers between devices  85.6 us (19%)
  matrix products  40.1 us (9%)
  other arithmetic  31.8 us (7%)
  starting transfers between devices  30.5 us (7%)
    psum x1, blocking collectives, body(): grad_sink = lax.psum(partial_2, 'ctx')  130 us
    all_to_all x1, waiting for transfers between devices, body(): lax.all_to_all(payload, 'ctx', split_axis=0, concat_axis=0, tiled=True)  84.3 us
    psum x1, blocking collectives, body(): partial_2 = lax.psum(sink_parts.reshape(head_count), 'dp')  21.8 us
    squeeze x20, local copies, waits for them, and re-layouts, body(): lax.map(partial(forward_group, scaling=scaling), (query_pairs, local_pair...  21.6 us
    dynamic_update_slice x15, local copies, waits for them, and re-layouts, body(): lax.map(partial(backward_group, scaling=scaling, seg_len=seg_len), (query...  11.9 us
    all_to_all x1, starting transfers between devices, body(): lax.all_to_all(payload, 'ctx', split_axis=0, concat_axis=0, tiled=True)  10.8 us
    all_to_all x1, starting transfers between devices, body(): lax.all_to_all(send_back.reshape(groups, capacity, BLOCK, double_dim), 'c...  9.92 us
    all_to_all x1, starting transfers between devices, body(): lax.all_to_all(sent_codes, 'ctx', split_axis=0, concat_axis=0, tiled=True)  9.8 us
  transfers between devices with their start and end apart: 3, of which 2 were waited for; matrix products, arithmetic and copies ran while one was open for 3% of the time, Pallas kernels for 0%

profile of v1, /device:TPU:354, one launch (start us, length us, event | category | flops | bytes accessed | tf_op | source)
XLA Modules:
  0.0 440.0 jit_solution(5020441362807392879)
XLA Ops:
  2.7 9.8 %all-to-all-start = ((s32[32,1,2]{2,1,0:T(1,128)}), s32[32,1,2]{2,1,0:T(1,128)S(1)}, u32[]{:S(2)}, u32[]{:S(2)}) async-start(s32[32,1,2]{2,1,0:T(1,128)} %bitcast.31), calls=%async_computation | async-start | bytes 32768 | tf_op jit(solution)/shard_map/all_to_all | solution.py:113
  12.5 1.5 reshape.729
  14.9 1.4 all-to-all-done
  16.6 2.8 gather_fusion
  19.4 10.8 %all-to-all-start.1 = ((bf16[32,2,128,256]{3,2,1,0:T(8,128)(2,1)}), bf16[32,2,128,256]{3,2,1,0:T(8,128)(2,1)}, u32[]{:S(2)}, u32[]{:S(2)}) async-start(bf16[32,2,128,256]{3,2,1,0:T(8,128)(2,1)} %bitcast.232), calls=%async_computation.1 | async-start | bytes 8388608 | tf_op jit(solution)/shard_map/all_to_all | solution.py:148
  31.5 1.1 copy.160
  32.6 2.2 copy.159
  34.8 1.5 copy.161
  36.3 84.3 %all-to-all-done.1 = bf16[32,2,128,256]{3,2,1,0:T(8,128)(2,1)} async-done(((bf16[32,2,128,256]{3,2,1,0:T(8,128)(2,1)}), bf16[32,2,128,256]{3,2,1,0:T(8,128)(2,1)}, u32[]{:S(2)}, u32[]{:S(2)}) %all-to-all-start.1) | async-done | bytes 4194336 | tf_op jit(solution)/shard_map/all_to_all | solution.py:148
  120.6 4.9 %gather_fusion.1 = bf16[60,128,256]{2,1,0:T(8,128)(2,1)} fusion(bf16[64,128,256]{2,1,0:T(8,128)(2,1)} %bitcast.36, s32[1024]{0:T(1024)S(1)} %pad_clamp_fusion.1), kind=kCustom, calls=%fused_computation.1 | custom fusion | bytes 7864560 | tf_op jit(solution)/shard_map/gather | solution.py:126
  125.5 4.4 %copy.155 = bf16[10,1,6,128,256]{4,3,2,0,1:T(8,128)(2,1)} copy(bf16[10,1,6,128,256]{4,3,0,2,1:T(8,128)(2,1)} %bitcast.235) | data formatting | bytes 7864320 | tf_op jit(solution)/shard_map/transpose | solution.py:127
  129.9 28.0 %while.28 = (s32[]{:T(128)}, bf16[5,2,1,256,128]{4,3,1,2,0:T(8,128)(2,1)}, f32[5,2,1,256]{3,1,2,0:T(2,128)S(1)}, bf16[5,2,1,256,128]{4,3,1,2,0:T(8,128)(2,1)}, b...) while((s32[]{:T(128)}, ...), condition=%wide.region_6.7_spmd, body=%wide.region_3.6_spmd.sunk | while | flops 274796032 | bytes 10773141 | solution.py:143
  130.9 1.2 dynamic-slice_bitcast_fusion.9
  132.1 1.4 multiply_reduce_fusion.6
  134.2 1.2 fusion.95
  136.5 1.2 dynamic-slice_bitcast_fusion.9
  137.7 1.4 multiply_reduce_fusion.6
  139.8 1.2 fusion.95
  142.1 1.2 dynamic-slice_bitcast_fusion.9
  143.3 1.4 multiply_reduce_fusion.6
  145.4 1.2 fusion.95
  147.7 1.2 dynamic-slice_bitcast_fusion.9
  148.9 1.4 multiply_reduce_fusion.6
  151.0 1.2 fusion.95
  153.3 1.2 dynamic-slice_bitcast_fusion.9
  154.5 1.4 multiply_reduce_fusion.6
  156.6 1.2 fusion.95
  157.9 69.4 %while.29 = (s32[]{:T(128)}, bf16[5,2,1,256,128]{3,4,1,0,2:T(8,128)(2,1)}, f32[5,2,1,256,256]{3,4,1,2,0:T(8,128)}, bf16[5,2,1,768,256]{4,3,1,0,2:T(8,128)(2,1)},...) while((s32[]{:T(128)}, ...), condition=%wide.region_10.11_spmd, body=%wide.region_7.10_spmd.sunk | while | flops 680788992 | bytes 27408636 | solution.py:150
  159.0 1.1 multiply_reduce_fusion.7
  161.3 1.2 dynamic-slice_bitcast_fusion.11
  162.5 1.3 fusion.107
  165.6 1.3 fusion.110
  168.6 1.4 copy.191
  172.9 1.1 multiply_reduce_fusion.7
  175.2 1.2 dynamic-slice_bitcast_fusion.11
  176.4 1.3 fusion.107
  179.5 1.3 fusion.110
  182.5 1.4 copy.191
  189.1 1.2 dynamic-slice_bitcast_fusion.11
  190.3 1.3 fusion.107
  193.4 1.3 fusion.110
  196.4 1.4 copy.191
  202.9 1.2 dynamic-slice_bitcast_fusion.11
  204.1 1.3 fusion.107
  207.3 1.3 fusion.110
  210.3 1.4 copy.191
  216.8 1.2 dynamic-slice_bitcast_fusion.11
  218.0 1.3 fusion.107
  221.1 1.3 fusion.110
  224.2 1.4 copy.191
  227.4 4.4 %copy.166 = bf16[6,10,1,128,256]{4,3,1,0,2:T(8,128)(2,1)} copy(bf16[6,10,1,128,256]{4,3,0,1,2:T(8,128)(2,1)} %bitcast.237) | data formatting | bytes 7864320 | tf_op jit(solution)/shard_map/transpose | solution.py:162
  231.8 4.9 %gather_fusion.2 = bf16[64,128,256]{2,1,0:T(8,128)(2,1)} fusion(bf16[60,128,256]{2,1,0:T(8,128)(2,1)} %bitcast.231, s32[1024]{0:T(1024)S(1)} %pad_clamp_fusion), kind=kCustom, calls=%fused_computation.2 | custom fusion | bytes 8388864 | tf_op jit(solution)/shard_map/gather | solution.py:166
  236.6 9.1 %broadcast_select_fusion = bf16[32,2,128,256]{3,1,2,0:T(2,128)(2,1)} fusion(pred[32,2]{1,0:T(8,128)(4,1)S(1)} %broadcast_in_dim.98, bf16[32,2,128,256]{3,2,1,0:T(8,128)(2,1)} %bitcast.234), kind=kLoop, calls=%fused_computation.85 | loop fusion | flops 2097152 | bytes 8388672 | tf_op jit(solution)/shard_map/jit(_where)/select_n | solution.py:166
  245.7 9.9 %all-to-all-start.2 = ((bf16[32,2,128,256]{3,1,2,0:T(2,128)(2,1)}), bf16[32,2,128,256]{3,1,2,0:T(2,128)(2,1)}, u32[]{:S(2)}, u32[]{:S(2)}) async-start(bf16[32,2,128,256]{3,1,2,0:T(2,128)(2,1)} %broadcast_select_fusion), calls=%async_computation.2 | async-start | bytes 8388608 | tf_op jit(solution)/shard_map/all_to_all | solution.py:167
  256.9 21.8 %psum.14 = f32[10]{0:T(128)S(1)} all-reduce(f32[10]{0:T(128)S(1)} %reshape.704), channel_id=1, replica_groups=mesh['dp'=16,'ctx'=32] {'dp'}, use_global_device_ids=true, to_apply=%region_12.13 | all-reduce | flops 10 | bytes 80 | tf_op jit(solution)/shard_map/psum | solution.py:194
  278.9 130.1 %psum.15 = f32[10]{0:T(128)} all-reduce(f32[10]{0:T(128)S(1)} %psum.14), channel_id=1, replica_groups=mesh['dp'=16,'ctx'=32] {'ctx'}, use_global_device_ids=true, to_apply=%region_13.14 | all-reduce | flops 10 | bytes 80 | tf_op jit(solution)/shard_map/psum | solution.py:195
  409.0 2.2 copy.170
  411.2 8.9 %copy.168 = bf16[32,2,128,256]{3,1,0,2:T(2,128)(2,1)} copy(bf16[32,2,128,256]{3,1,2,0:T(2,128)(2,1)} %all-to-all-done.2) | data formatting | bytes 8388608 | tf_op jit(solution)/shard_map/all_to_all | solution.py:167
  420.0 7.2 %reshape.728 = bf16[64,128,256,1]{2,0,1,3:T(8,128)(2,1)} reshape(bf16[32,2,128,256]{3,1,0,2:T(2,128)(2,1)} %copy.168) | data formatting | bytes 8388608 | tf_op jit(solution)/shard_map/reshape | solution.py:181
  427.3 4.9 %fusion.56 = f32[10,2,128,256]{3,0,2,1:T(8,128)} fusion(bf16[64,128,256,1]{2,0,1,3:T(8,128)(2,1)} %reshape.728, s32[10,2]{0,1:T(2,128)S(1)} %multiply_add_fusion, s32[64]{0:T(128)S(1)} %eq.67), kind=kOutput, calls=%fused_computation.97 | convolution fusion | flops 83887360 | bytes 6816080 | tf_op jit(solution)/shard_map/pj,pbe->jbe/dot_general | solution.py:178
  432.2 3.4 copy.169
  435.6 2.2 fusion.53
  437.9 1.1 copy.172
  438.9 1.1 copy.171
  (163 shorter events, 55.6 us)
Async XLA Ops:
  0.6 0.7 copy-start
  0.6 13.5 %copy-start.3 = (bf16[1,256,1280]{2,1,0:T(8,128)(2,1)S(1)}, bf16[1,256,1280]{2,1,0:T(8,128)(2,1)}, u32[]{:S(2)}) copy-start(bf16[1,256,1280]{2,1,0:T(8,128)(2,1)} %param.12) | copy-start | bytes 1966084
  2.7 13.6 %all-to-all-start = ((s32[32,1,2]{2,1,0:T(1,128)}), s32[32,1,2]{2,1,0:T(1,128)S(1)}, u32[]{:S(2)}, u32[]{:S(2)}) async-start(s32[32,1,2]{2,1,0:T(1,128)} %bitcast.31), calls=%async_computation | async-start | bytes 32768 | tf_op jit(solution)/shard_map/all_to_all | solution.py:113
  19.4 11.0 %copy-start.2 = (bf16[1,256,1280]{2,1,0:T(8,128)(2,1)S(1)}, bf16[1,256,1280]{2,1,0:T(8,128)(2,1)}, u32[]{:S(2)}) copy-start(bf16[1,256,1280]{2,1,0:T(8,128)(2,1)} %param.11) | copy-start | bytes 1966084
  19.4 101.2 %all-to-all-start.1 = ((bf16[32,2,128,256]{3,2,1,0:T(8,128)(2,1)}), bf16[32,2,128,256]{3,2,1,0:T(8,128)(2,1)}, u32[]{:S(2)}, u32[]{:S(2)}) async-start(bf16[32,2,128,256]{3,2,1,0:T(8,128)(2,1)} %bitcast.232), calls=%async_computation.1 | async-start | bytes 8388608 | tf_op jit(solution)/shard_map/all_to_all | solution.py:148
  30.1 0.8 copy-start.5
  30.1 1.1 copy-start.4
  245.7 165.4 %all-to-all-start.2 = ((bf16[32,2,128,256]{3,1,2,0:T(2,128)(2,1)}), bf16[32,2,128,256]{3,1,2,0:T(2,128)(2,1)}, u32[]{:S(2)}, u32[]{:S(2)}) async-start(bf16[32,2,128,256]{3,1,2,0:T(2,128)(2,1)} %broadcast_select_fusion), calls=%async_computation.2 | async-start | bytes 8388608 | tf_op jit(solution)/shard_map/all_to_all | solution.py:167
  435.6 4.5 %copy-start.1 = (s32[10,1,6]{0,1,2:T(1,128)S(1)}, s32[10,1,6]{0,1,2:T(1,128)}, u32[]{:S(2)}) copy-start(s32[10,1,6]{0,1,2:T(1,128)} %param.14) | copy-start | bytes 724
